TPU v7x, 32 devices: a whole 2x2x4 slice. The times are simulated.
32 devices in a mesh: row: 8 (over z, y), col: 4 (over x, core).
Axes of the slice: x: 2, y: 2, z: 4, core: 2. Of those that a mesh axis runs over, the one named last changes fastest.
Arguments:
- nodes: bfloat16 [10240, 512], P(('row', 'col')), may hold values from -6 to 6
- edges: bfloat16 [65536, 512], P(('row', 'col')), may hold values from -6 to 6
- sender_slot: int32 [65536], P(('row', 'col')), may hold values from 0 to 575, as said below
- receiver: int32 [65536], P(('row', 'col')), may hold values from 0 to 319
- send_list: int32 [32, 256], P(('row', 'col')), may hold values from 0 to 319
- w_edge_in: bfloat16 [1536, 512], replicated, may hold values from -0.15625 to 0.15625
- b_edge: float32 [512], replicated, may hold values from -4 to 4
- w_edge_out: bfloat16 [512, 512], replicated, may hold values from -1 to 1
- g_edge: float32 [512], replicated, may hold values from 0.1 to 1.9
- w_node_in: bfloat16 [1024, 512], replicated, may hold values from -0.1875 to 0.1875
- b_node: float32 [512], replicated, may hold values from -4 to 4
- w_node_out: bfloat16 [512, 512], replicated, may hold values from -1 to 1
- g_node: float32 [512], replicated, may hold values from 0.1 to 1.9
- grad_nodes_out: bfloat16 [10240, 512], P(('row', 'col')), may hold values from -6 to 6
- grad_edges_out: bfloat16 [65536, 512], P(('row', 'col')), may hold values from -6 to 6
Outputs:
- new_nodes: bfloat16 [10240, 512], P(('row', 'col'))
- new_edges: bfloat16 [65536, 512], P(('row', 'col'))
- grad_nodes: float32 [10240, 512], P(('row', 'col'))
- grad_edges: bfloat16 [65536, 512], P(('row', 'col'))
Inputs may be any that keep to these rules, and one draw needn't show every extreme that they name: `sender_slot`: A value 320 + p * 8 + c on an edge of device d never has p = d.
All inputs are finite; a program needn't handle non-finite values.
Results may differ from a plain program's by a relative error of at most 0.0085.
Values may be sent and summed in bfloat16 or wider, within the bound.
A program may use at most 128 MiB of HBM per device.

v0:
```python
import jax
import jax.numpy as jnp
from jax import lax
from jax.sharding import PartitionSpec as P

norm_eps = 1e-05


def perceptron(pieces, weight_in, bias_vec, weight_out, gain_vec):
    joined = jnp.concatenate(pieces, axis=1)
    pre_act = jnp.dot(joined, weight_in, preferred_element_type=jnp.float32) + bias_vec
    activated = jax.nn.silu(pre_act).astype(jnp.bfloat16)
    hidden = jnp.dot(activated, weight_out, preferred_element_type=jnp.float32)
    row_mean = jnp.mean(hidden, axis=-1, keepdims=True)
    centred = hidden - row_mean
    variance = jnp.mean(centred * centred, axis=-1, keepdims=True)
    inv_std = lax.rsqrt(variance + norm_eps)
    normed = centred * inv_std
    return (pre_act, normed, inv_std, normed * gain_vec)


def perceptron_grad(upstream, pre_act, normed, inv_std, weight_out, gain_vec):
    scaled = upstream * gain_vec
    d_hidden = inv_std * (
        scaled
        - jnp.mean(scaled, axis=-1, keepdims=True)
        - normed * jnp.mean(scaled * normed, axis=-1, keepdims=True)
    )
    d_hidden = d_hidden.astype(jnp.bfloat16)
    d_act = jnp.dot(d_hidden, weight_out.T, preferred_element_type=jnp.float32)
    sigmoid_v = jax.nn.sigmoid(pre_act)
    return (d_act * sigmoid_v * (1.0 + pre_act * (1.0 - sigmoid_v))).astype(jnp.bfloat16)


def selector(indices, width):
    return (indices[:, None] == jnp.arange(width, dtype=jnp.int32)[None, :]).astype(jnp.bfloat16)


def split_halves(values):
    upper = values.astype(jnp.bfloat16)
    lower = (values - upper.astype(jnp.float32)).astype(jnp.bfloat16)
    return (upper, lower)


def pick_rows(picker, table):
    return jnp.dot(picker, table, preferred_element_type=jnp.float32)


def pick_rows_exact(picker, table):
    upper, lower = split_halves(table)
    return pick_rows(picker, upper) + pick_rows(picker, lower)


def gather_sum(picker, values):
    return lax.dot_general(
        picker, values, (((0,), (0,)), ((), ())), preferred_element_type=jnp.float32
    )


def gather_sum_exact(picker, values):
    upper, lower = split_halves(values)
    return gather_sum(picker, upper) + gather_sum(picker, lower)


def local(
    nodes,
    edges,
    sender_slot,
    receiver,
    send_list,
    w_edge_in,
    b_edge,
    w_edge_out,
    g_edge,
    w_node_in,
    b_node,
    w_node_out,
    g_node,
    grad_nodes_out,
    grad_edges_out,
):
    row_count = lax.axis_size("row")
    col_count = lax.axis_size("col")
    peer_count = row_count * col_count
    node_rows, feature_width = nodes.shape
    listing = send_list[0]
    slot_count = listing.shape[0] // peer_count
    table_rows = node_rows + peer_count * slot_count
    listing_pick = selector(listing, node_rows)
    outgoing = (
        pick_rows(listing_pick, nodes)
        .astype(jnp.bfloat16)
        .reshape(peer_count, slot_count, feature_width)
    )
    arrived = lax.all_to_all(outgoing, ("row", "col"), split_axis=0, concat_axis=0, tiled=True)
    row_table = jnp.concatenate(
        [nodes, arrived.reshape(peer_count * slot_count, feature_width)], axis=0
    )
    slot_pick = selector(sender_slot, table_rows)
    receiver_pick = selector(receiver, node_rows)
    senders = pick_rows(slot_pick, row_table).astype(jnp.bfloat16)
    targets = pick_rows(receiver_pick, nodes).astype(jnp.bfloat16)
    pre_edge, normed_edge, inv_edge, message = perceptron(
        [edges, senders, targets], w_edge_in, b_edge, w_edge_out, g_edge
    )
    new_edges = (edges.astype(jnp.float32) + message).astype(jnp.bfloat16)
    incoming = gather_sum_exact(receiver_pick, message).astype(jnp.bfloat16)
    pre_node, normed_node, inv_node, update = perceptron(
        [nodes, incoming], w_node_in, b_node, w_node_out, g_node
    )
    new_nodes = (nodes.astype(jnp.float32) + update).astype(jnp.bfloat16)
    d_pre_node = perceptron_grad(
        grad_nodes_out.astype(jnp.float32), pre_node, normed_node, inv_node, w_node_out, g_node
    )
    d_node_in = jnp.dot(d_pre_node, w_node_in.T, preferred_element_type=jnp.float32)
    d_own = d_node_in[:, :feature_width]
    d_incoming = d_node_in[:, feature_width:]
    d_message = grad_edges_out.astype(jnp.float32) + pick_rows_exact(receiver_pick, d_incoming)
    d_pre_edge = perceptron_grad(d_message, pre_edge, normed_edge, inv_edge, w_edge_out, g_edge)
    d_self = jnp.dot(d_pre_edge, w_edge_in[:feature_width].T, preferred_element_type=jnp.float32)
    d_to = jnp.dot(d_pre_edge, w_edge_in[2 * feature_width :].T, preferred_element_type=jnp.float32)
    per_slot = gather_sum(slot_pick, d_pre_edge)
    remote_sums = per_slot[node_rows:].reshape(peer_count, slot_count, feature_width)
    returned = lax.all_to_all(
        remote_sums.astype(jnp.bfloat16), ("row", "col"), split_axis=0, concat_axis=0, tiled=True
    ).astype(remote_sums.dtype)
    owned_sums = per_slot[:node_rows] + gather_sum_exact(
        listing_pick, returned.reshape(peer_count * slot_count, feature_width)
    )
    sender_block = w_edge_in[feature_width : 2 * feature_width].T
    upper, lower = split_halves(owned_sums)
    d_from_nodes = jnp.dot(upper, sender_block, preferred_element_type=jnp.float32) + jnp.dot(
        lower, sender_block, preferred_element_type=jnp.float32
    )
    grad_nodes = (
        grad_nodes_out.astype(jnp.float32)
        + d_own
        + gather_sum_exact(receiver_pick, d_to)
        + d_from_nodes
    )
    grad_edges = (grad_edges_out.astype(jnp.float32) + d_self).astype(jnp.bfloat16)
    return (new_nodes, new_edges, grad_nodes, grad_edges)


def solution(mesh):
    in_specs = (
        P(("row", "col"), None),
        P(("row", "col"), None),
        P(("row", "col")),
        P(("row", "col")),
        P(("row", "col"), None),
        P(),
        P(),
        P(),
        P(),
        P(),
        P(),
        P(),
        P(),
        P(("row", "col"), None),
        P(("row", "col"), None),
    )
    out_specs = (
        P(("row", "col"), None),
        P(("row", "col"), None),
        P(("row", "col"), None),
        P(("row", "col"), None),
    )
    return jax.shard_map(local, mesh=mesh, in_specs=in_specs, out_specs=out_specs, check_vma=False)
```

profile of v0, /device:TPU:0, one launch (start us, length us, event | category | flops | bytes accessed | tf_op | source)
XLA Modules:
  0.0 87.2 jit_solution(5087801274334364698)
XLA Ops:
  0.6 0.0 copy-start
  0.6 2.1 %fusion.51 = bf16[32,8,512]{2,1,0:T(8,128)(2,1)} fusion(bf16[320,512]{1,0:T(8,128)(2,1)} %param.15, s32[256]{0:T(256)} %bitcast.25), kind=kOutput, calls=%fused_computation.65 | convolution fusion | flops 84099072 | bytes 590848 | tf_op jit(solution)/shard_map/dot_general | solution.py:46
  2.8 7.5 %all-to-all-start = ((bf16[32,8,512]{2,1,0:T(8,128)(2,1)}), bf16[32,8,512]{2,1,0:T(8,128)(2,1)}, u32[]{:S(2)}, u32[]{:S(2)}) async-start(bf16[32,8,512]{2,1,0:T(8,128)(2,1)} %fusion.51), calls=%async_computation | async-start | bytes 524288 | tf_op jit(solution)/shard_map/all_to_all | solution.py:95
  10.2 0.0 copy-start.10
  10.3 0.0 copy-start.13
  10.3 3.0 %copy.20 = bf16[2048,512]{0,1:T(8,128)(2,1)S(1)} copy(bf16[2048,512]{1,0:T(8,128)(2,1)} %param.29) | data formatting | bytes 4194304 | tf_op args[14]
  13.2 3.9 %copy.19 = bf16[2048,512]{0,1:T(8,128)(2,1)} copy(bf16[2048,512]{1,0:T(8,128)(2,1)} %param.16) | data formatting | bytes 4194304 | tf_op args[1]
  17.2 0.0 copy-done.10
  17.2 0.0 copy-done.13
  17.2 2.5 %fusion.15 = bf16[2048,512]{1,0:T(8,128)(2,1)} fusion(bf16[320,512]{1,0:T(8,128)(2,1)S(1)} %copy-done.10, s32[2048]{0:T(1024)S(1)} %copy-done.13), kind=kOutput, calls=%fused_computation.30 | convolution fusion | flops 672792576 | bytes 2433024 | tf_op jit(solution)/shard_map/dot_general | solution.py:46
  19.7 1.1 %all-to-all-done = bf16[32,8,512]{2,1,0:T(8,128)(2,1)} async-done(((bf16[32,8,512]{2,1,0:T(8,128)(2,1)}), bf16[32,8,512]{2,1,0:T(8,128)(2,1)}, u32[]{:S(2)}, u32[]{:S(2)}) %all-to-all-start) | async-done | bytes 262176 | tf_op jit(solution)/shard_map/all_to_all | solution.py:95
  20.8 0.0 copy-done.20
  20.8 3.4 %fusion.16 = bf16[2048,512]{1,0:T(8,128)(2,1)S(1)} fusion(s32[2048]{0:T(1024)S(1)} %copy-done.20, bf16[256,512]{1,0:T(8,128)(2,1)} %bitcast.2, bf16[320,512]{1,0:T(8,128)(2,1)S(1)} %copy-done.10), kind=kOutput, calls=%fused_computation.31 | convolution fusion | flops 1211367424 | bytes 2695168 | tf_op jit(solution)/shard_map/dot_general | solution.py:46
  24.2 0.0 copy-done.6
  24.2 0.0 copy-done.7
  24.2 0.0 copy-done.24
  24.2 0.0 copy-start.18
  24.2 0.0 copy-start.22
  24.2 3.4 %fusion = f32[2048,512]{1,0:T(8,128)S(1)} fusion(bf16[1536,512]{1,0:T(8,128)(2,1)S(1)} %copy-done.7, bf16[2048,512]{1,0:T(8,128)(2,1)S(1)} %copy-done.24, bf16[2048,512]{1,0:T(8,128)(2,1)S(1)} %fusion.16, bf16[2048,512]{1,0:T(8,128)(2,1)S(1)} %copy-done.6), kind=kOutput, calls=%fused_computation | convolution fusion | flops 3240099840 | bytes 12058624 | tf_op jit(solution)/shard_map/dot_general | solution.py:11
  27.7 0.0 copy-done.18
  27.7 0.0 copy-done.22
  27.7 1.6 %fusion.106 = (f32[2048]{0:T(1024)S(1)}, f32[2048,512]{0,1:T(8,128)S(1)}) fusion(bf16[512,512]{1,0:T(8,128)(2,1)S(1)} %copy-done.18, f32[2048,512]{1,0:T(8,128)S(1)} %fusion, f32[512]{0:T(512)S(1)} %copy-done.22), kind=kOutput, calls=%fused_computation.134 | convolution fusion | flops 1081079808 | bytes 8923136 | tf_op jit(solution)/shard_map/dot_general | solution.py:13
  29.3 0.3 copy-done.25
  29.7 0.5 multiply_reduce_fusion.1
  30.2 0.1 copy-done.16
  30.3 1.7 %fusion.17 = f32[320,512]{1,0:T(8,128)S(1)} fusion(f32[2048,512]{0,1:T(8,128)S(1)} %get-tuple-element.15, f32[512]{0:T(512)S(1)} %copy-done.16, f32[2048]{0:T(1024)S(1)} %add_rsqrt_fusion, f32[2048]{0:T(1024)S(1)} %broadcast_multiply_fusion.2, s32[2048]{0:T(1024)S(1)} %copy-done.13), kind=kOutput, calls=%fused_computation.32 | convolution fusion | flops 676593664 | bytes 4876288 | tf_op jit(solution)/shard_map/dot_general | solution.py:55
  32.0 0.0 copy-done.1
  32.0 0.0 copy-start.11
  32.0 0.0 copy-start.21
  32.0 0.0 copy-start.17
  32.0 1.7 %fusion.46 = bf16[320,512]{1,0:T(8,128)(2,1)S(1)} fusion(f32[320,512]{1,0:T(8,128)S(1)} %fusion.17, f32[2048,512]{0,1:T(8,128)S(1)} %get-tuple-element.15, f32[512]{0:T(512)S(1)} %copy-done.16, f32[2048]{0:T(1024)S(1)} %add_rsqrt_fusion, f32[2048]{0:T(1024)S(1)} %broadcast_multiply_fusion.2, s32[2048]{0:T(1024)S(1)} %copy-done.13), kind=kOutput, calls=%fused_computation.61 | convolution fusion | flops 680067072 | bytes 5203968 | tf_op jit(solution)/shard_map/dot_general | solution.py:55
  33.8 0.0 copy-start.9
  33.8 0.0 copy-start.15
  33.9 0.5 convolution_add_fusion.2
  34.4 0.0 copy-start.23
  34.4 0.5 fusion.107
  34.9 0.2 multiply_reduce_fusion.2
  35.1 0.1 copy-done.23
  35.2 0.5 copy-done.5
  35.7 0.0 copy-done.15
  35.7 1.0 %fusion.56 = (f32[320]{0:T(512)S(1)}, f32[320]{0:T(512)S(1)}, bf16[320,512]{1,0:T(8,128)(2,1)}) fusion(bf16[320,512]{1,0:T(8,128)(2,1)S(1)} %copy-done.9, f32[512]{0:T(512)S(1)} %copy-done.15, f32[320]{0:T(512)S(1)} %add_rsqrt_fusion.1, f32[320,512]{1,0:T(8,128)S(1)} %get-tuple-element.17, f32[320]{0:T(512)S(1)} %broadcast_multiply_fusion.5, ...), kind=kLoop, calls=%fused_computation.72 | loop fusion | flops 1801600 | bytes 1645568 | tf_op jit(solution)/shard_map/reduce_sum | solution.py:26
  36.7 3.6 %fusion.50 = f32[320,1024]{1,0:T(8,128)} fusion(bf16[1024,512]{1,0:T(8,128)(2,1)S(1)} %copy-done, bf16[512,512]{1,0:T(8,128)(2,1)} %param.26, f32[320,512]{1,0:T(8,128)} %copy-done.23, bf16[320,512]{1,0:T(8,128)(2,1)S(1)} %copy-done.9, f32[320,512]{1,0:T(8,128)} %copy-done.5, f32[320]{0:T(512)S(1)} %get-tuple-element.19, f32[320]{0:T(512)S(1)} %get-tuple-element.20, ...), kind=kOutput, calls=%fused_computation.64 | convolution fusion | flops 506265600 | bytes 4529152 | tf_op jit(solution)/shard_map/dot_general | solution.py:115
  40.3 2.7 %fusion.11 = f32[2048,512]{0,1:T(8,128)S(1)} fusion(s32[2048]{0:T(1024)S(1)} %copy-done.13, f32[320,1024]{1,0:T(8,128)} %fusion.50), kind=kOutput, calls=%fused_computation.26 | convolution fusion | flops 671744000 | bytes 4530176 | tf_op jit(solution)/shard_map/dot_general | solution.py:46
  43.0 0.4 copy-done.3
  43.4 5.7 %fusion.105 = (f32[2048]{0:T(1024)S(1)}, f32[2048]{0:T(1024)S(1)}, bf16[2048,512]{0,1:T(8,128)(2,1)}, f32[2048,512]{0,1:T(8,128)S(1)}) fusion(f32[2048]{0:T(1024)S(1)} %add_rsqrt_fusion, f32[2048,512]{0,1:T(8,128)S(1)} %copy-done.2, f32[2048]{0:T(1024)S(1)} %broadcast_multiply_fusion.2, f32[512]{0:T(512)S(1)} %copy-done.16, ...), kind=kOutput, calls=%fused_computation.133 | convolution fusion | flops 686026752 | bytes 19572736 | tf_op jit(solution)/shard_map/dot_general | solution.py:46
  49.0 0.0 copy-done.19
  49.1 0.0 copy-start.8
  49.1 2.8 %multiply_convert_fusion = bf16[2048,512]{1,0:T(8,128)(2,1)S(1)} fusion(f32[2048,512]{1,0:T(8,128)S(1)} %copy-done.26, bf16[512,512]{1,0:T(8,128)(2,1)S(1)} %copy-done.19, f32[2048,512]{0,1:T(8,128)S(1)} %get-tuple-element.18, f32[2048,512]{0,1:T(8,128)S(1)} %copy-done.2, f32[2048]{0:T(1024)S(1)} %broadcast_multiply_fusion, ...), kind=kOutput, calls=%fused_computation.14 | convolution fusion | flops 1091567616 | bytes 15239168 | tf_op jit(solution)/shard_map/dot_general | solution.py:30
  51.9 2.6 %fusion.9 = bf16[2048,512]{0,1:T(8,128)(2,1)} fusion(bf16[2048,512]{0,1:T(8,128)(2,1)S(1)} %copy.20, bf16[2048,512]{1,0:T(8,128)(2,1)S(1)} %multiply_convert_fusion, bf16[1536,512]{1,0:T(8,128)(2,1)S(1)} %copy-done.8), kind=kOutput, calls=%fused_computation.12 | convolution fusion | flops 1076887552 | bytes 6815744 | tf_op jit(solution)/shard_map/dot_general | solution.py:120
  54.5 2.0 %fusion.6 = f32[576,512]{1,0:T(8,128)S(1)} fusion(bf16[2048,512]{1,0:T(8,128)(2,1)S(1)} %multiply_convert_fusion, s32[2048]{0:T(1024)S(1)} %copy-done.20), kind=kOutput, calls=%fused_computation.9 | convolution fusion | flops 1209139200 | bytes 3284992 | tf_op jit(solution)/shard_map/dot_general | solution.py:55
  56.5 3.2 %fusion.71 = f32[2048,512]{1,0:T(8,128)} fusion(bf16[2048,512]{1,0:T(8,128)(2,1)S(1)} %multiply_convert_fusion, bf16[1536,512]{1,0:T(8,128)(2,1)S(1)} %copy-done.8), kind=kOutput, calls=%fused_computation.97 | convolution fusion | flops 1073741824 | bytes 6815744 | tf_op jit(solution)/shard_map/dot_general | solution.py:121
  59.8 0.7 fusion.91
  60.5 4.7 %all-to-all-start.1 = ((bf16[32,8,512]{2,1,0:T(8,128)(2,1)}), bf16[32,8,512]{2,1,0:T(8,128)(2,1)S(1)}, u32[]{:S(2)}, u32[]{:S(2)}) async-start(bf16[32,8,512]{2,1,0:T(8,128)(2,1)} %fusion.91), calls=%async_computation.1 | async-start | bytes 524288 | tf_op jit(solution)/shard_map/all_to_all | solution.py:124
  65.2 0.0 copy-start.4
  65.2 5.9 %fusion.12 = f32[320,512]{1,0:T(8,128)} fusion(f32[2048,512]{1,0:T(8,128)} %fusion.71, s32[2048]{0:T(1024)S(1)} %copy-done.13), kind=kOutput, calls=%fused_computation.27 | convolution fusion | flops 675938304 | bytes 4857856 | tf_op jit(solution)/shard_map/dot_general | solution.py:55
  71.1 3.9 %copy.23 = bf16[2048,512]{1,0:T(8,128)(2,1)} copy(bf16[2048,512]{0,1:T(8,128)(2,1)} %fusion.9) | data formatting | bytes 4194304
  75.0 2.5 %copy.22 = bf16[2048,512]{1,0:T(8,128)(2,1)} copy(bf16[2048,512]{0,1:T(8,128)(2,1)S(1)} %copy-done.4) | data formatting | bytes 4194304
  77.5 4.1 %fusion.42 = f32[320,512]{1,0:T(8,128)S(1)} fusion(f32[320,512]{1,0:T(8,128)} %fusion.12, s32[2048]{0:T(1024)S(1)} %copy-done.13, f32[2048,512]{1,0:T(8,128)} %fusion.71, bf16[320,512]{1,0:T(8,128)(2,1)} %param.28, f32[320,1024]{1,0:T(8,128)} %fusion.50), kind=kOutput, calls=%fused_computation.59 | convolution fusion | flops 673447936 | bytes 6496256 | tf_op jit(solution)/shard_map/dot_general | solution.py:55
  81.6 0.0 all-to-all-done.1
  81.6 0.0 copy-done.14
  81.6 0.4 fusion.76
  82.0 1.5 %fusion.41 = f32[320,512]{1,0:T(8,128)S(1)} fusion(f32[320,512]{1,0:T(8,128)S(1)} %fusion.76, f32[576,512]{1,0:T(8,128)} %copy-done.12, bf16[32,8,512]{2,1,0:T(8,128)(2,1)S(1)} %all-to-all-done.1, s32[256]{0:T(256)S(1)} %bitcast.27), kind=kOutput, calls=%fused_computation.57 | convolution fusion | flops 84688896 | bytes 2229248 | tf_op jit(solution)/shard_map/dot_general | solution.py:55
  83.5 1.4 %fusion.74 = f32[320,512]{1,0:T(8,128)S(1)} fusion(bf16[1536,512]{1,0:T(8,128)(2,1)} %param.20, f32[320,512]{1,0:T(8,128)S(1)} %fusion.41), kind=kOutput, calls=%fused_computation.100 | convolution fusion | flops 167936000 | bytes 1835008 | tf_op jit(solution)/shard_map/dot_general | solution.py:132
  84.9 2.3 %fusion.40 = f32[320,512]{1,0:T(8,128)} fusion(f32[320,512]{1,0:T(8,128)S(1)} %fusion.42, f32[320,512]{1,0:T(8,128)S(1)} %fusion.74, bf16[1536,512]{1,0:T(8,128)(2,1)} %param.20, f32[320,512]{1,0:T(8,128)S(1)} %fusion.41), kind=kOutput, calls=%fused_computation.55 | convolution fusion | flops 168755200 | bytes 3145728 | tf_op jit(solution)/shard_map/dot_general | solution.py:132
  (31 shorter events, 0.1 us)
Async XLA Ops:
  0.6 33.2 %copy-start = (bf16[1024,512]{1,0:T(8,128)(2,1)S(1)}, bf16[1024,512]{1,0:T(8,128)(2,1)}, u32[]{:S(2)}) copy-start(bf16[1024,512]{1,0:T(8,128)(2,1)} %param.24) | copy-start | bytes 3145732
  2.8 18.0 %all-to-all-start = ((bf16[32,8,512]{2,1,0:T(8,128)(2,1)}), bf16[32,8,512]{2,1,0:T(8,128)(2,1)}, u32[]{:S(2)}, u32[]{:S(2)}) async-start(bf16[32,8,512]{2,1,0:T(8,128)(2,1)} %fusion.51), calls=%async_computation | async-start | bytes 524288 | tf_op jit(solution)/shard_map/all_to_all | solution.py:95
  10.2 6.9 %copy-start.10 = (bf16[320,512]{1,0:T(8,128)(2,1)S(1)}, bf16[320,512]{1,0:T(8,128)(2,1)}, u32[]{:S(2)}) copy-start(bf16[320,512]{1,0:T(8,128)(2,1)} %param.15) | copy-start | bytes 983044
  10.3 6.9 %copy-start.13 = (s32[2048]{0:T(1024)S(1)}, s32[2048]{0:T(1024)}, u32[]{:S(2)}) copy-start(s32[2048]{0:T(1024)} %param.18) | copy-start | bytes 24580
  17.2 3.6 %copy-start.20 = (s32[2048]{0:T(1024)S(1)}, s32[2048]{0:T(1024)}, u32[]{:S(2)}) copy-start(s32[2048]{0:T(1024)} %param.17) | copy-start | bytes 24580
  20.8 3.4 %copy-start.6 = (bf16[2048,512]{1,0:T(8,128)(2,1)S(1)}, bf16[2048,512]{1,0:T(8,128)(2,1)}, u32[]{:S(2)}) copy-start(bf16[2048,512]{1,0:T(8,128)(2,1)} %param.16) | copy-start | bytes 6291460
  20.8 3.4 %copy-start.7 = (bf16[1536,512]{1,0:T(8,128)(2,1)S(1)}, bf16[1536,512]{1,0:T(8,128)(2,1)}, u32[]{:S(2)}) copy-start(bf16[1536,512]{1,0:T(8,128)(2,1)} %param.20) | copy-start | bytes 4718596
  20.8 3.4 %copy-start.24 = (bf16[2048,512]{1,0:T(8,128)(2,1)S(1)}, bf16[2048,512]{1,0:T(8,128)(2,1)}, u32[]{:S(2)}) copy-start(bf16[2048,512]{1,0:T(8,128)(2,1)} %fusion.15) | copy-start | bytes 6291460
  24.2 3.5 %copy-start.18 = (bf16[512,512]{1,0:T(8,128)(2,1)S(1)}, bf16[512,512]{1,0:T(8,128)(2,1)}, u32[]{:S(2)}) copy-start(bf16[512,512]{1,0:T(8,128)(2,1)} %param.22) | copy-start | bytes 1572868
  24.2 3.5 %copy-start.22 = (f32[512]{0:T(512)S(1)}, f32[512]{0:T(512)}, u32[]{:S(2)}) copy-start(f32[512]{0:T(512)} %param.21) | copy-start | bytes 6148
  27.7 2.0 %copy-start.25 = (f32[2048,512]{1,0:T(8,128)}, f32[2048,512]{1,0:T(8,128)S(1)}, u32[]{:S(2)}) copy-start(f32[2048,512]{1,0:T(8,128)S(1)} %fusion) | copy-start | bytes 12582916
  29.7 2.3 %copy-start.1 = (f32[2048,512]{0,1:T(8,128)}, f32[2048,512]{0,1:T(8,128)S(1)}, u32[]{:S(2)}) copy-start(f32[2048,512]{0,1:T(8,128)S(1)} %get-tuple-element.15) | copy-start | bytes 12582916
  29.7 0.7 copy-start.16
  32.0 1.8 %copy-start.11 = (bf16[320,512]{1,0:T(8,128)(2,1)S(1)}, bf16[320,512]{1,0:T(8,128)(2,1)}, u32[]{:S(2)}) copy-start(bf16[320,512]{1,0:T(8,128)(2,1)} %param.15) | copy-start | bytes 983044
  32.0 1.8 %copy-start.21 = (f32[512]{0:T(512)S(1)}, f32[512]{0:T(512)}, u32[]{:S(2)}) copy-start(f32[512]{0:T(512)} %param.25) | copy-start | bytes 6148
  32.0 2.3 %copy-start.17 = (bf16[512,512]{1,0:T(8,128)(2,1)S(1)}, bf16[512,512]{1,0:T(8,128)(2,1)}, u32[]{:S(2)}) copy-start(bf16[512,512]{1,0:T(8,128)(2,1)} %param.26) | copy-start | bytes 1572868
  33.8 1.9 %copy-start.9 = (bf16[320,512]{1,0:T(8,128)(2,1)S(1)}, bf16[320,512]{1,0:T(8,128)(2,1)}, u32[]{:S(2)}) copy-start(bf16[320,512]{1,0:T(8,128)(2,1)} %param.28) | copy-start | bytes 983044
  33.8 1.9 %copy-start.15 = (f32[512]{0:T(512)S(1)}, f32[512]{0:T(512)}, u32[]{:S(2)}) copy-start(f32[512]{0:T(512)} %param.27) | copy-start | bytes 6148
  34.4 0.8 copy-start.23
  34.9 0.8 copy-start.5
  40.3 2.7 %copy-start.2 = (f32[2048,512]{0,1:T(8,128)S(1)}, f32[2048,512]{0,1:T(8,128)}, u32[]{:S(2)}) copy-start(f32[2048,512]{0,1:T(8,128)} %copy-done.1) | copy-start | bytes 12582916
  40.3 3.1 %copy-start.3 = (bf16[2048,512]{0,1:T(8,128)(2,1)S(1)}, bf16[2048,512]{0,1:T(8,128)(2,1)}, u32[]{:S(2)}) copy-start(bf16[2048,512]{0,1:T(8,128)(2,1)} %copy.19) | copy-start | bytes 6291460
  43.4 5.7 %copy-start.19 = (bf16[512,512]{1,0:T(8,128)(2,1)S(1)}, bf16[512,512]{1,0:T(8,128)(2,1)}, u32[]{:S(2)}) copy-start(bf16[512,512]{1,0:T(8,128)(2,1)} %param.22) | copy-start | bytes 1572868
  43.4 5.7 %copy-start.26 = (f32[2048,512]{1,0:T(8,128)S(1)}, f32[2048,512]{1,0:T(8,128)}, u32[]{:S(2)}) copy-start(f32[2048,512]{1,0:T(8,128)} %copy-done.25) | copy-start | bytes 12582916
  49.1 2.8 %copy-start.8 = (bf16[1536,512]{1,0:T(8,128)(2,1)S(1)}, bf16[1536,512]{1,0:T(8,128)(2,1)}, u32[]{:S(2)}) copy-start(bf16[1536,512]{1,0:T(8,128)(2,1)} %param.20) | copy-start | bytes 4718596
  56.5 3.2 %copy-start.12 = (f32[576,512]{1,0:T(8,128)}, f32[576,512]{1,0:T(8,128)S(1)}, u32[]{:S(2)}) copy-start(f32[576,512]{1,0:T(8,128)S(1)} %fusion.6) | copy-start | bytes 3538948
  60.5 21.1 %all-to-all-start.1 = ((bf16[32,8,512]{2,1,0:T(8,128)(2,1)}), bf16[32,8,512]{2,1,0:T(8,128)(2,1)S(1)}, u32[]{:S(2)}, u32[]{:S(2)}) async-start(bf16[32,8,512]{2,1,0:T(8,128)(2,1)} %fusion.91), calls=%async_computation.1 | async-start | bytes 524288 | tf_op jit(solution)/shard_map/all_to_all | solution.py:124
  65.2 9.8 %copy-start.4 = (bf16[2048,512]{0,1:T(8,128)(2,1)S(1)}, bf16[2048,512]{0,1:T(8,128)(2,1)}, u32[]{:S(2)}) copy-start(bf16[2048,512]{0,1:T(8,128)(2,1)} %get-tuple-element.12) | copy-start | bytes 6291460
  77.5 4.1 %copy-start.14 = (s32[1,256]{1,0:T(1,128)S(1)}, s32[1,256]{1,0:T(1,128)}, u32[]{:S(2)}) copy-start(s32[1,256]{1,0:T(1,128)} %param.19) | copy-start | bytes 3076
where the time goes:
time: 87.8 us; the launch traced here: 87.2 us
  matrix products  55.5 us (63%)
  local copies, waits for them, and re-layouts  15.6 us (18%)
  starting transfers between devices  12.2 us (14%)
  other arithmetic  1.81 us (2%)
  waiting for transfers between devices  1.1 us (1%)
  between operations  1.04 us (1%)
    dot_general x7, matrix products, gather_sum(): lax.dot_general(picker, values, (((0,), (0,)), ((), ())), preferred_eleme...  17.2 us
    dot_general x5, matrix products, pick_rows(): return jnp.dot(picker, table, preferred_element_type=jnp.float32)  16.4 us
    unnamed x58, local copies, waits for them, and re-layouts  14.8 us
    all_to_all x1, starting transfers between devices, local(): lax.all_to_all(outgoing, ('row', 'col'), split_axis=0, concat_axis=0, til...  7.45 us
    all_to_all x1, starting transfers between devices, local(): lax.all_to_all(remote_sums.astype(jnp.bfloat16), ('row', 'col'), split_ax...  4.7 us
    dot_general x2, matrix products, perceptron(): jnp.dot(joined, weight_in, preferred_element_type=jnp.float32) + bias_vec  3.94 us
    dot_general x1, matrix products, local(): jnp.dot(d_pre_node, w_node_in.T, preferred_element_type=jnp.float32)  3.58 us
    dot_general x1, matrix products, local(): jnp.dot(d_pre_edge, w_edge_in[2 * feature_width:].T, preferred_element_ty...  3.24 us
  transfers between devices with their start and end apart: 2, of which 1 were waited for; matrix products, arithmetic and copies ran while one was open for 30% of the time, Pallas kernels for 0%

commit v1 on v0

v1 whole, which is shorter than its diff:
```python
import functools

import jax
import jax.numpy as jnp
from jax import lax
from jax.experimental import pallas as pl
from jax.experimental.pallas import tpu as pltpu
from jax.sharding import PartitionSpec as P

norm_eps = 1e-05
LANES = 128
TILE = 256
MESH = pl.DeviceIdType.MESH
f32 = jnp.float32
bf16 = jnp.bfloat16


def mm(left, right):
    return jnp.dot(left, right, preferred_element_type=f32)


def mm_t(left, right):
    return lax.dot_general(left, right, (((1,), (1,)), ((), ())), preferred_element_type=f32)


def sigmoid(value):
    return 0.5 * jnp.tanh(0.5 * value) + 0.5


def row_mean(value):
    return jnp.mean(value, axis=-1, keepdims=True)


def normalize(value):
    centred = value - row_mean(value)
    inv_std = lax.rsqrt(row_mean(centred * centred) + norm_eps)
    return centred * inv_std, inv_std


def norm_grad(upstream, gain, normed, inv_std):
    scaled = upstream * gain
    return (inv_std * (scaled - row_mean(scaled) - normed * row_mean(scaled * normed))).astype(bf16)


def ones_where(mask):
    return jnp.where(mask, 1.0, 0.0).astype(bf16)


def as_column(row):
    return jnp.transpose(jnp.broadcast_to(row, (LANES, row.shape[1])))


def kernel(
    sizes,
    nodes, slot, recv, listing, b_e, g_e, b_n, g_n, gno,
    edges, geo, w_ei_h, w_eo_h, w_ni_h, w_no_h,
    new_nodes, grad_nodes, new_edges, grad_edges,
    ebuf, gbuf, w_ei, w_eo, w_ni, w_no, npad, table, picks, picks_t,
    pre_s, nrm_s, inv_s, nebuf, dpbuf, inc, dinc, racc, lacc,
    outgoing, arrived, sums, returned,
    sem_w, sem_e, sem_g, sem_ne, sem_ge, send1, recv1, send2, recv2,
):
    rows, cols, cap = sizes
    peers = rows * cols
    n, d = nodes.shape
    tiles, _, tile = slot.shape
    remote = peers * cap
    width = remote + 2 * n
    n_pad = npad.shape[0]
    my_row, my_col = lax.axis_index("row"), lax.axis_index("col")
    me = my_row * cols + my_col

    def span(t):
        return pl.ds(pl.multiple_of(t * tile, tile), tile)

    def coords(k):
        peer = lax.rem(me + k, peers)
        return peer, (peer // cols, lax.rem(peer, cols))

    barrier = pltpu.get_barrier_semaphore()

    def greet(k, carry):
        pl.semaphore_signal(barrier, inc=1, device_id=coords(k)[1], device_id_type=MESH)
        return carry

    lax.fori_loop(1, peers, greet, 0)

    def load_edges(t):
        return pltpu.make_async_copy(edges.at[span(t)], ebuf.at[span(t)], sem_e.at[t])

    def load_grads(t):
        return pltpu.make_async_copy(geo.at[span(t)], gbuf.at[span(t)], sem_g.at[t])

    def store_edges(t):
        return pltpu.make_async_copy(nebuf.at[span(t)], new_edges.at[span(t)], sem_ne.at[t])

    def store_grads(t):
        return pltpu.make_async_copy(gbuf.at[span(t)], grad_edges.at[span(t)], sem_ge.at[t])

    load_w = [
        pltpu.make_async_copy(src, dst, sem_w.at[i])
        for i, (src, dst) in enumerate(((w_ei_h, w_ei), (w_eo_h, w_eo), (w_ni_h, w_ni), (w_no_h, w_no)))
    ]
    load_w[0].start()
    for t in range(tiles):
        load_edges(t).start()
    for copy in load_w[1:]:
        copy.start()
    for t in range(tiles):
        load_grads(t).start()

    npad[:n] = nodes[...]
    if n_pad > n:
        npad[n:] = jnp.zeros((n_pad - n, d), bf16)
        dinc[n:] = jnp.zeros((n_pad - n, d), bf16)
    lists = listing[...]
    list_col = as_column(lists)
    lane = lax.broadcasted_iota(jnp.int32, (remote, LANES), 1)
    list_pick = jnp.concatenate(
        [ones_where(lane + k == list_col) for k in range(0, n_pad, LANES)], axis=1
    )
    outgoing[...] = mm(list_pick, npad[...]).reshape(peers, cap, d).astype(bf16)
    arrived[me] = jnp.zeros((cap, d), bf16)
    returned[me] = jnp.zeros((cap, d), bf16)
    inc[...] = jnp.zeros_like(inc)
    racc[...] = jnp.zeros_like(racc)
    lacc[...] = jnp.zeros_like(lacc)

    def exchange(src, dst, send, got):
        def push(k, carry):
            peer, where = coords(k)
            pltpu.make_async_remote_copy(
                src_ref=src.at[peer], dst_ref=dst.at[me], send_sem=send, recv_sem=got,
                device_id=where, device_id_type=MESH,
            ).start()
            return carry

        lax.fori_loop(1, peers, push, 0)

    def whole(src, dst, send, got):
        part = pl.ds(0, peers - 1)
        return pltpu.make_async_remote_copy(
            src_ref=src.at[part], dst_ref=dst.at[part], send_sem=send, recv_sem=got,
            device_id=coords(1)[1], device_id_type=MESH,
        )

    pl.semaphore_wait(barrier, peers - 1)
    exchange(outgoing, arrived, send1, recv1)

    load_w[0].wait()
    table[remote : remote + n] = mm(nodes[...], w_ei[2 * d :]).astype(bf16)
    table[remote + n :] = mm(nodes[...], w_ei[d : 2 * d]).astype(bf16)

    def first(t, carry):
        sender = slot[t]
        c1 = jnp.where(sender >= n, sender - n, sender + (remote + n))
        c2 = recv[t] + remote
        rows_at = lax.broadcasted_iota(jnp.int32, (width, tile), 0)
        picks_t[t] = ones_where((rows_at == c1) | (rows_at == c2))
        c1c, c2c = as_column(c1), as_column(c2)
        lanes_at = lax.broadcasted_iota(jnp.int32, (tile, LANES), 1)
        for k in range(0, width, LANES):
            if k < remote:
                mask = lanes_at + k == c1c
            else:
                mask = (lanes_at + k == c1c) | (lanes_at + k == c2c)
            picks[span(t), k : k + LANES] = ones_where(mask)
        load_edges(t).wait()
        pre_s[span(t)] = (
            mm(ebuf[span(t)], w_ei[:d]) + mm(picks[span(t), remote:], table[remote:]) + b_e[...]
        )
        return carry

    lax.fori_loop(0, tiles, first, 0)

    whole(outgoing, arrived, send1, recv1).wait_recv()
    landed = arrived[...].astype(f32).reshape(remote, d).astype(bf16)
    table[:remote] = mm(landed, w_ei[d : 2 * d]).astype(bf16)
    load_w[1].wait()

    def second(t, carry):
        pre = pre_s[span(t)] + mm(picks[span(t), :remote], table[:remote])
        q = sigmoid(pre)
        pre_s[span(t)] = q * (1.0 + pre * (1.0 - q))
        normed, inv_std = normalize(mm((pre * q).astype(bf16), w_eo[...]))
        nrm_s[span(t)] = normed
        inv_s[span(t)] = inv_std
        message = normed * g_e[...]
        nebuf[span(t)] = (ebuf[span(t)].astype(f32) + message).astype(bf16)
        store_edges(t).start()
        inc[...] += mm(picks_t[t, remote : remote + n], message.astype(bf16))
        return carry

    lax.fori_loop(0, tiles, second, 0)

    load_w[2].wait()
    load_w[3].wait()
    pre = mm(nodes[...], w_ni[:d]) + mm(inc[...].astype(bf16), w_ni[d:]) + b_n[...]
    q = sigmoid(pre)
    normed, inv_std = normalize(mm((pre * q).astype(bf16), w_no[...]))
    new_nodes[...] = (nodes[...].astype(f32) + normed * g_n[...]).astype(bf16)
    given = gno[...].astype(f32)
    d_mid = norm_grad(given, g_n[...], normed, inv_std)
    d_pre = (mm_t(d_mid, w_no[...]) * (q * (1.0 + pre * (1.0 - q)))).astype(bf16)
    dinc[:n] = mm_t(d_pre, w_ni[d:]).astype(bf16)
    grad_nodes[...] = given + mm_t(d_pre, w_ni[:d])

    def third(t, carry):
        load_grads(t).wait()
        upstream = gbuf[span(t)].astype(f32) + mm(picks[span(t), remote : remote + n_pad], dinc[...])
        d_hid = norm_grad(upstream, g_e[...], nrm_s[span(t)], inv_s[span(t)])
        d_in = (mm_t(d_hid, w_eo[...]) * pre_s[span(t)]).astype(bf16)
        dpbuf[span(t)] = d_in
        racc[...] += mm(picks_t[t, :remote], d_in)
        return carry

    lax.fori_loop(0, tiles, third, 0)
    sums[...] = racc[...].reshape(peers, cap, d).astype(bf16)
    exchange(sums, returned, send2, recv2)

    def fourth(t, carry):
        d_in = dpbuf[span(t)]
        gbuf[span(t)] = (gbuf[span(t)].astype(f32) + mm_t(d_in, w_ei[:d])).astype(bf16)
        store_grads(t).start()
        lacc[...] += mm(picks_t[t, remote:], d_in)
        return carry

    lax.fori_loop(0, tiles, fourth, 0)
    grad_nodes[...] += mm_t(lacc[:n].astype(bf16), w_ei[2 * d :])

    whole(sums, returned, send2, recv2).wait_recv()
    back = returned[...].astype(f32).reshape(remote, d).astype(bf16)
    list_pick_t = ones_where(lax.broadcasted_iota(jnp.int32, (n, remote), 0) == lists)
    owned = lacc[n:] + mm(list_pick_t, back)
    grad_nodes[...] += mm_t(owned.astype(bf16), w_ei[d : 2 * d])

    whole(outgoing, arrived, send1, recv1).wait_send()
    whole(sums, returned, send2, recv2).wait_send()
    for t in range(tiles):
        store_edges(t).wait()
        store_grads(t).wait()


def local(
    nodes, edges, sender_slot, receiver, send_list, w_edge_in, b_edge, w_edge_out, g_edge,
    w_node_in, b_node, w_node_out, g_node, grad_nodes_out, grad_edges_out,
):
    rows, cols = lax.axis_size("row"), lax.axis_size("col")
    peers = rows * cols
    n, d = nodes.shape
    e = edges.shape[0]
    cap = send_list.shape[1] // peers
    remote = peers * cap
    width = remote + 2 * n
    tile = TILE
    tiles = e // tile
    n_pad = -(-n // LANES) * LANES
    assert e % tile == 0 and remote % LANES == 0 and width % LANES == 0 and n_pad <= 2 * n
    vmem = pl.BlockSpec(memory_space=pltpu.VMEM)
    hbm = pl.BlockSpec(memory_space=pl.ANY)
    dma = pltpu.SemaphoreType.DMA
    new_nodes, grad_nodes, new_edges, grad_edges = pl.pallas_call(
        functools.partial(kernel, (rows, cols, cap)),
        out_shape=(
            jax.ShapeDtypeStruct((n, d), bf16),
            jax.ShapeDtypeStruct((n, d), f32),
            jax.ShapeDtypeStruct((e, d), bf16),
            jax.ShapeDtypeStruct((e, d), bf16),
        ),
        in_specs=[vmem] * 9 + [hbm] * 6,
        out_specs=(vmem, vmem, hbm, hbm),
        scratch_shapes=[
            pltpu.VMEM((e, d), bf16),
            pltpu.VMEM((e, d), bf16),
            pltpu.VMEM(w_edge_in.shape, bf16),
            pltpu.VMEM(w_edge_out.shape, bf16),
            pltpu.VMEM(w_node_in.shape, bf16),
            pltpu.VMEM(w_node_out.shape, bf16),
            pltpu.VMEM((n_pad, d), bf16),
            pltpu.VMEM((width, d), bf16),
            pltpu.VMEM((e, width), bf16),
            pltpu.VMEM((tiles, width, tile), bf16),
            pltpu.VMEM((e, d), f32),
            pltpu.VMEM((e, d), f32),
            pltpu.VMEM((e, 1), f32),
            pltpu.VMEM((e, d), bf16),
            pltpu.VMEM((e, d), bf16),
            pltpu.VMEM((n, d), f32),
            pltpu.VMEM((n_pad, d), bf16),
            pltpu.VMEM((remote, d), f32),
            pltpu.VMEM((2 * n, d), f32),
            pltpu.VMEM((peers, cap, d), bf16),
            pltpu.VMEM((peers, cap, d), bf16),
            pltpu.VMEM((peers, cap, d), bf16),
            pltpu.VMEM((peers, cap, d), bf16),
            dma((4,)),
            dma((tiles,)),
            dma((tiles,)),
            dma((tiles,)),
            dma((tiles,)),
            dma, dma, dma, dma,
        ],
        compiler_params=pltpu.CompilerParams(
            collective_id=0, has_side_effects=True, vmem_limit_bytes=60 * 1024 * 1024
        ),
        name="round",
    )(
        nodes,
        sender_slot.reshape(tiles, 1, tile),
        receiver.reshape(tiles, 1, tile),
        send_list,
        b_edge.reshape(1, d),
        g_edge.reshape(1, d),
        b_node.reshape(1, d),
        g_node.reshape(1, d),
        grad_nodes_out,
        edges, grad_edges_out, w_edge_in, w_edge_out, w_node_in, w_node_out,
    )
    return new_nodes, new_edges, grad_nodes, grad_edges


def solution(mesh):
    split = P(("row", "col"), None)
    flat = P(("row", "col"))
    whole = P()
    in_specs = (split, split, flat, flat, split) + (whole,) * 8 + (split, split)
    return jax.shard_map(
        local, mesh=mesh, in_specs=in_specs, out_specs=(split,) * 4, check_vma=False
    )
```

time: 87.8 us -> 48 us (0.55)
  matrix products: 55.5 us -> 0 us
  Pallas kernels: 0 us -> 40.1 us
  starting transfers between devices: 12.2 us -> 0 us
  local copies, waits for them, and re-layouts: 15.6 us -> 7.08 us
  other arithmetic: 1.81 us -> 0 us
  waiting for transfers between devices: 1.1 us -> 0 us
    dot_general x22 -> x0, matrix products: 55.5 us -> none  [the longest x7 17.2 us: gather_sum(): lax.dot_general(picker, values, (((0,), (0,)), ((), ())), preferred_eleme...]
    pallas_call x0 -> x1, Pallas kernels: none -> 40.1 us  [local(): pl.pallas_call(functools.partial(kernel, (rows, cols, cap)), out_shape=(j...]
    all_to_all x2 -> x0, starting transfers between devices: 12.2 us -> none  [the longest x1 7.45 us: local(): lax.all_to_all(outgoing, ('row', 'col'), split_axis=0, concat_axis=0, til...]
    unnamed x58 -> x8, local copies, waits for them, and re-layouts: 14.8 us -> 7.08 us
    reduce_sum x3 -> x0, other arithmetic: 1.78 us -> none  [the longest x1 1.02 us: perceptron_grad(): jnp.mean(scaled, axis=-1, keepdims=True)]
    all_to_all x2 -> x0, waiting for transfers between devices: 1.1 us -> none  [the longest x1 1.1 us: local(): lax.all_to_all(outgoing, ('row', 'col'), split_axis=0, concat_axis=0, til...]
  transfers between devices with their start and end apart: 2 -> 0, of which waited for: 1 -> 0; matrix products, arithmetic and copies ran while one was open for 30% -> 0% of each run, Pallas kernels for 0% -> 0%
where the time goes in v1:
time: 48 us; the launch traced here: 47.8 us
  Pallas kernels  40.1 us (84%)
  local copies, waits for them, and re-layouts  7.08 us (15%)
  between operations  0.65 us (1%)
    pallas_call x1, Pallas kernels, local(): pl.pallas_call(functools.partial(kernel, (rows, cols, cap)), out_shape=(j...  40.1 us
    unnamed x8, local copies, waits for them, and re-layouts  7.08 us

profile of v1, /device:TPU:0, one launch (start us, length us, event | category | flops | bytes accessed | tf_op | source)
XLA Modules:
  0.0 47.8 jit_solution(35398126609187057)
XLA Ops:
  0.6 40.1 %round.1 = (bf16[320,512]{1,0:T(8,128)(2,1)}, f32[320,512]{1,0:T(8,128)}, bf16[2048,512]{1,0:T(8,128)(2,1)}, bf16[2048,512]{1,0:T(8,128)(2,1)}) custom-call(bf16[320,512]{1,0:T(8,128)(2,1)} %nodes.1, s32[8,1,256]{2,1,0:T(1,128)} %bitcast.6, s32[8,1,256]{2,1,0:T(1,128)} %bitcast.7, s32[1,256]{1,0:T(1,128)} %listing.1, f32[1,512]{1,0:T(1,128)} %bitcast.8, ...), custom_call_target="tpu_custom_call" | custom-call | tf_op jit(solution)/shard_map/round/pallas_call | solution.py:262
  40.8 1.7 %copy.23 = bf16[320,512]{1,0:T(8,128)(2,1)} copy(bf16[320,512]{1,0:T(8,128)(2,1)} %get-tuple-element.16) | data formatting | bytes 655360
  42.5 0.0 copy-start.1
  42.5 0.0 copy-start
  42.5 3.2 %copy.24 = bf16[2048,512]{1,0:T(8,128)(2,1)} copy(bf16[2048,512]{1,0:T(8,128)(2,1)} %get-tuple-element.17) | data formatting | bytes 4194304
  45.7 0.0 copy-done.1
  45.7 0.8 %copy.25 = f32[320,512]{1,0:T(8,128)} copy(f32[320,512]{1,0:T(8,128)S(1)} %copy-done.1) | data formatting | bytes 1310720
  46.5 0.0 copy-done
  46.5 1.3 %copy.26 = bf16[2048,512]{1,0:T(8,128)(2,1)} copy(bf16[2048,512]{1,0:T(8,128)(2,1)S(1)} %copy-done) | data formatting | bytes 4194304
Async XLA Ops:
  42.5 3.2 %copy-start.1 = (f32[320,512]{1,0:T(8,128)S(1)}, f32[320,512]{1,0:T(8,128)}, u32[]{:S(2)}) copy-start(f32[320,512]{1,0:T(8,128)} %get-tuple-element.18) | copy-start | bytes 1966084
  42.5 4.0 %copy-start = (bf16[2048,512]{1,0:T(8,128)(2,1)S(1)}, bf16[2048,512]{1,0:T(8,128)(2,1)}, u32[]{:S(2)}) copy-start(bf16[2048,512]{1,0:T(8,128)(2,1)} %get-tuple-element.19) | copy-start | bytes 6291460

commit v2 on v1

--- a/solution.py
+++ b/solution.py
@@ -9,7 +9,8 @@
 
 norm_eps = 1e-05
 LANES = 128
-TILE = 256
+TILE = 512
+CHUNK = 512
 MESH = pl.DeviceIdType.MESH
 f32 = jnp.float32
 bf16 = jnp.bfloat16
@@ -239,6 +240,26 @@
     for t in range(tiles):
         store_edges(t).wait()
         store_grads(t).wait()
+
+
+def deliver(count, *refs):
+    held, finals = refs[:count], refs[count : 2 * count]
+    bufs, got, put = refs[2 * count : 3 * count], refs[3 * count], refs[3 * count + 1]
+    loads, stores = [], []
+    for source, final, buf in zip(held, finals, bufs):
+        total = source.shape[0]
+        step = CHUNK if total % CHUNK == 0 else total
+        for at in range(0, total, step):
+            part, i = pl.ds(at, step), len(loads)
+            loads.append(pltpu.make_async_copy(source.at[part], buf.at[part], got.at[i]))
+            stores.append(pltpu.make_async_copy(buf.at[part], final.at[part], put.at[i]))
+    for load in loads:
+        load.start()
+    for load, store in zip(loads, stores):
+        load.wait()
+        store.start()
+    for store in stores:
+        store.wait()
 
 
 def local(
@@ -316,6 +337,16 @@
         grad_nodes_out,
         edges, grad_edges_out, w_edge_in, w_edge_out, w_node_in, w_node_out,
     )
+    results = (new_edges, grad_edges, new_nodes, grad_nodes)
+    parts = sum(r.shape[0] // CHUNK if r.shape[0] % CHUNK == 0 else 1 for r in results)
+    new_edges, grad_edges, new_nodes, grad_nodes = pl.pallas_call(
+        functools.partial(deliver, len(results)),
+        out_shape=tuple(jax.ShapeDtypeStruct(r.shape, r.dtype) for r in results),
+        in_specs=[hbm] * len(results),
+        out_specs=(hbm,) * len(results),
+        scratch_shapes=[pltpu.VMEM(r.shape, r.dtype) for r in results] + [dma((parts,)), dma((parts,))],
+        name="deliver",
+    )(*results)
     return new_nodes, new_edges, grad_nodes, grad_edges
 
 

time: 48 us -> 41 us (0.85)
  local copies, waits for them, and re-layouts: 7.08 us -> 0 us
    unnamed x8 -> x0, local copies, waits for them, and re-layouts: 7.08 us -> none
    pallas_call x0 -> x1, Pallas kernels: none -> 4.7 us  [local(): pl.pallas_call(functools.partial(deliver, len(results)), out_shape=tuple(...]
    pallas_call x1, Pallas kernels: 40.1 us -> 35.5 us  [local(): pl.pallas_call(functools.partial(kernel, (rows, cols, cap)), out_shape=(j...]
where the time goes in v2:
time: 41 us; the launch traced here: 40.9 us
  Pallas kernels  40.2 us (98%)
  between operations  0.65 us (2%)
    pallas_call x1, Pallas kernels, local(): pl.pallas_call(functools.partial(kernel, (rows, cols, cap)), out_shape=(j...  35.5 us
    pallas_call x1, Pallas kernels, local(): pl.pallas_call(functools.partial(deliver, len(results)), out_shape=tuple(...  4.7 us

profile of v2, /device:TPU:0, one launch (start us, length us, event | category | flops | bytes accessed | tf_op | source)
XLA Modules:
  0.0 40.9 jit_solution(4389428753008849482)
XLA Ops:
  0.6 35.5 %round.1 = (bf16[320,512]{1,0:T(8,128)(2,1)}, f32[320,512]{1,0:T(8,128)}, bf16[2048,512]{1,0:T(8,128)(2,1)}, bf16[2048,512]{1,0:T(8,128)(2,1)}) custom-call(bf16[320,512]{1,0:T(8,128)(2,1)} %nodes.1, s32[4,1,512]{2,1,0:T(1,128)} %bitcast.6, s32[4,1,512]{2,1,0:T(1,128)} %bitcast.7, s32[1,256]{1,0:T(1,128)} %listing.1, f32[1,512]{1,0:T(1,128)} %bitcast.8, ...), custom_call_target="tpu_custom_call" | custom-call | tf_op jit(solution)/shard_map/round/pallas_call | solution.py:283
  36.2 4.7 %deliver.1 = (bf16[2048,512]{1,0:T(8,128)(2,1)}, bf16[2048,512]{1,0:T(8,128)(2,1)}, bf16[320,512]{1,0:T(8,128)(2,1)}, f32[320,512]{1,0:T(8,128)}) custom-call(bf16[2048,512]{1,0:T(8,128)(2,1)} %get-tuple-element.12.refs_0_, bf16[2048,512]{1,0:T(8,128)(2,1)} %get-tuple-element.13.refs_1_, bf16[320,512]{1,0:T(8,128)(2,1)} %get-tuple-element.14.refs_2_, ...), custom_call_target="tpu_custom_call" | custom-call | tf_op jit(solution)/shard_map/deliver/pallas_call | solution.py:342
